TPU v7x, 32 devices: a whole 2x2x4 slice. The times are simulated.
32 devices in a mesh: row: 8 (over z, core), col: 4 (over y, x).
Axes of the slice: x: 2, y: 2, z: 4, core: 2. Of those that a mesh axis runs over, the one named last changes fastest.
Arguments:
- gram: bfloat16 [32768, 32768], P('row', 'col'), may hold values from -1 to 5, as said below
- start_basis: bfloat16 [32768, 256], P(('row', 'col')), may hold values from -12 to 12
- slab: float32 [32768, 4096], P('row', 'col'), may hold values from -6 to 6
Outputs:
- core_scaled: float32 [32768, 256], P(('row', 'col'))
- next_unfolding: float32 [4096, 256], P(('row', 'col'))
Inputs may be any that keep to these rules, and one draw needn't show every extreme that they name: gram is symmetric: entry (i, j) equals entry (j, i).
All inputs are finite; a program needn't handle non-finite values.
Results may differ from a plain program's by a relative error of at most 0.003.
Values may be sent and summed in bfloat16 or wider, within the bound.
A program may use at most 192 MiB of HBM per device.

v0:
```python
import math
import jax
import jax.numpy as jnp
from jax import lax
from jax.sharding import PartitionSpec as P

N = 32768
NMODE = 16


def body(gram, start_basis, slab):
    col_count = lax.axis_size("col")
    highest = lax.Precision.HIGHEST
    contract_rows = (((0,), (0,)), ((), ()))
    own_rows = lax.all_gather(start_basis, "col", axis=0, tiled=True)
    first_image = lax.psum_scatter(
        lax.dot_general(gram, own_rows, contract_rows, preferred_element_type=jnp.float32),
        "row",
        scatter_dimension=0,
        tiled=True,
    ).astype(jnp.bfloat16)
    col_rows = lax.all_gather(first_image, "row", axis=0, tiled=True)
    second_image = lax.psum_scatter(
        jnp.dot(gram, col_rows, preferred_element_type=jnp.float32),
        "col",
        scatter_dimension=0,
        tiled=True,
    )
    own_gram = lax.dot_general(
        second_image,
        second_image,
        contract_rows,
        precision=highest,
        preferred_element_type=jnp.float32,
    )
    small_gram = lax.psum(own_gram, ("row", "col"))
    factor = jnp.linalg.cholesky(small_gram)
    basis_cols = jax.scipy.linalg.solve_triangular(factor, second_image.T, lower=True).T
    block_basis = lax.all_gather(basis_cols, "col", axis=0, tiled=True)
    own_proj = lax.psum_scatter(
        lax.dot_general(
            block_basis, slab, contract_rows, precision=highest, preferred_element_type=jnp.float32
        ),
        "row",
        scatter_dimension=0,
        tiled=True,
    )
    core_out = basis_cols * math.sqrt(N)
    mode_share = NMODE // col_count
    grouped = own_proj.reshape(own_proj.shape[0], mode_share, own_proj.shape[1] // mode_share)
    regrouped = lax.all_to_all(grouped, "col", split_axis=0, concat_axis=1, tiled=True)
    return (
        core_out,
        regrouped.reshape(regrouped.shape[0] * regrouped.shape[1], regrouped.shape[2]),
    )


def solution(mesh):
    in_specs = (P("row", "col"), P(("row", "col"), None), P("row", "col"))
    out_specs = (P(("row", "col"), None), P(("row", "col"), None))
    return jax.shard_map(body, mesh=mesh, in_specs=in_specs, out_specs=out_specs, check_vma=False)
```

profile of v0, /device:TPU:0, one launch (start us, length us, event | category | flops | bytes accessed | tf_op | source)
XLA Modules:
  0.0 614.0 jit_solution(10611750755675535246)
XLA Ops:
  7.2 0.0 all-gather.4.cloned.1.call-start
  7.2 0.7 all-gather.4.cloned.1.call-update
  7.9 0.0 reduce-scatter.4.cloned.1.call-start
  7.9 39.8 %all-gather.4.cloned.1.call-done = bf16[4096,256]{1,0:T(8,128)(2,1)} async-done(((bf16[1024,256]{1,0:T(8,128)(2,1)}), bf16[4096,256]{1,0:T(8,128)(2,1)}) %all-gather.4.cloned.1.call-update) | async-done | bytes 2097168 | tf_op jit(solution)/shard_map/all_gather | solution.py:15
  47.8 30.0 %fusion.9 = f32[8192,256]{1,0:T(8,128)} fusion(bf16[4096,8192]{1,0:T(8,128)(2,1)} %param.3, bf16[4096,256]{1,0:T(8,128)(2,1)} %all-gather.4.cloned.1.call-done), kind=kOutput, calls=%fused_computation.32 | convolution fusion | flops 17179869184 | bytes 77594624 | tf_op jit(solution)/shard_map/dot_general | solution.py:17
  77.7 0.0 reduce-scatter.4.cloned.1.call-update
  77.7 0.0 all-gather.6.cloned.1.call-start
  77.8 89.6 %reduce-scatter.4.cloned.1.call-done = f32[1024,256]{1,0:T(8,128)} async-done(((f32[8192,256]{1,0:T(8,128)}), f32[1024,256]{1,0:T(8,128)}) %reduce-scatter.4.cloned.1.call-update) | async-done | bytes 1048592 | tf_op jit(solution)/shard_map/reduce_scatter | solution.py:16
  167.4 2.1 convert_element_type.3
  169.5 0.0 all-gather.6.cloned.1.call-update
  169.5 0.0 reduce-scatter.6.cloned.1.call-start
  169.6 45.4 %all-gather.6.cloned.1.call-done = bf16[8192,256]{1,0:T(8,128)(2,1)} async-done(((bf16[1024,256]{1,0:T(8,128)(2,1)}), bf16[8192,256]{1,0:T(8,128)(2,1)}) %all-gather.6.cloned.1.call-update) | async-done | bytes 4194320 | tf_op jit(solution)/shard_map/all_gather | solution.py:22
  215.0 29.2 %convolution_bitcast_fusion = f32[4096,256]{0,1:T(8,128)} fusion(bf16[8192,256]{1,0:T(8,128)(2,1)} %all-gather.6.cloned.1.call-done, bf16[4096,8192]{1,0:T(8,128)(2,1)} %param.3), kind=kOutput, calls=%fused_computation.2 | convolution fusion | flops 17179869184 | bytes 75497472 | tf_op jit(solution)/shard_map/dot_general | solution.py:24
  244.2 0.0 reduce-scatter.6.cloned.1.call-update
  244.2 0.0 all-reduce.3.cloned.1.call-start
  244.3 51.5 %reduce-scatter.6.cloned.1.call-done = f32[1024,256]{0,1:T(8,128)} async-done(((f32[4096,256]{0,1:T(8,128)}), f32[1024,256]{0,1:T(8,128)}) %reduce-scatter.6.cloned.1.call-update) | async-done | bytes 1048592 | tf_op jit(solution)/shard_map/reduce_scatter | solution.py:23
  295.8 0.0 copy-start
  295.8 3.4 fusion.10
  299.1 0.0 all-reduce.3.cloned.1.call-update
  299.1 0.2 all-gather.8.cloned.1.call-start
  299.4 128.9 %all-reduce.3.cloned.1.call-done = f32[256,256]{0,1:T(8,128)} async-done(((f32[256,256]{0,1:T(8,128)}), f32[256,256]{0,1:T(8,128)}) %all-reduce.3.cloned.1.call-update) | async-done | bytes 262160 | tf_op jit(solution)/shard_map/psum | solution.py:36
  428.3 1.1 copy.6
  429.4 1.0 fusion.2
  430.4 11.7 %cholesky.50 = f32[128,128]{1,0:T(8,128)S(1)} custom-call(f32[128,128]{1,0:T(8,128)S(1)} %cholesky.118), custom_call_target="Cholesky" | custom-call | tf_op jit(solution)/shard_map/jit(cholesky)/cholesky | solution.py:37
  442.1 9.8 %custom-call.15 = f32[1,128,128]{1,2,0:T(8,128)S(1)} custom-call(f32[1,128,128]{2,1,0:T(8,128)S(1)} %get-tuple-element.25), custom_call_target="InvertDiagBlocksLowerTriangular" | custom-call | tf_op jit(solution)/shard_map/jit(cholesky)/cholesky | solution.py:37
  452.0 0.2 constant_dynamic-update-slice_fusion.1
  452.2 0.3 convolution_subtract_fusion.1
  452.4 11.7 %cholesky.105 = f32[128,128]{1,0:T(8,128)S(1)} custom-call(f32[128,128]{1,0:T(8,128)S(1)} %convolution_subtract_fusion.1), custom_call_target="Cholesky" | custom-call | tf_op jit(solution)/shard_map/jit(cholesky)/cholesky | solution.py:37
  464.2 0.7 compare_reduce_fusion
  466.3 0.1 triangular_solve.57
  466.4 4.3 while.1
  466.6 0.6 fusion.25
  467.1 1.4 bitcast_dynamic-update-slice_fusion.2
  468.6 0.6 fusion.25
  469.2 1.4 bitcast_dynamic-update-slice_fusion.2
  470.6 19.7 %custom-call.16 = f32[2,128,128]{1,2,0:T(8,128)S(1)} custom-call(f32[2,128,128]{2,1,0:T(8,128)S(1)} %get-tuple-element.9), custom_call_target="InvertDiagBlocksLowerTriangular" | custom-call | tf_op jit(solution)/shard_map/jit(_solve_triangular)/triangular_solve | solution.py:38
  490.3 0.0 copy-done
  490.3 0.6 fusion
  491.0 0.6 convolution_subtract_fusion
  491.6 0.6 fusion.4
  492.2 1.0 maximum_bitcast_fusion
  493.2 0.0 all-gather.8.cloned.1.call-update
  493.3 0.0 reduce-scatter.8.cloned.1.call-start
  493.3 51.7 %all-gather.8.cloned.1.call-done = f32[4096,256]{0,1:T(8,128)} async-done(((f32[1024,256]{0,1:T(8,128)}), f32[4096,256]{0,1:T(8,128)}) %all-gather.8.cloned.1.call-update) | async-done | bytes 4194320 | tf_op jit(solution)/shard_map/all_gather | solution.py:39
  545.1 18.3 %fusion.11 = f32[256,1024]{1,0:T(8,128)} fusion(f32[4096,256]{0,1:T(8,128)} %all-gather.8.cloned.1.call-done, f32[4096,1024]{1,0:T(8,128)} %param.5), kind=kOutput, calls=%fused_computation.34 | convolution fusion | flops 12884901888 | bytes 22020096 | tf_op jit(solution)/shard_map/dot_general | solution.py:41
  563.3 0.0 reduce-scatter.8.cloned.1.call-update
  563.3 32.8 %reduce-scatter.8.cloned.1.call-done = f32[32,1024]{1,0:T(8,128)} async-done(((f32[256,1024]{1,0:T(8,128)}), f32[32,1024]{1,0:T(8,128)}) %reduce-scatter.8.cloned.1.call-update) | async-done | bytes 131088 | tf_op jit(solution)/shard_map/reduce_scatter | solution.py:40
  596.1 1.6 reshape.30
  597.7 3.7 all-to-all-start
  601.4 0.1 broadcast_multiply_fusion
  601.5 1.3 copy.8
  602.9 3.6 all-to-all-done
  606.4 0.7 reshape.31
  (10 shorter events, 0.2 us)
Async XLA Ops:
  7.2 40.6 %all-gather.4.cloned.1.call-start = ((), (), s32[]{:S(2)}) async-start(), calls=%async_computation.4 | async-start | bytes 2621440 | tf_op jit(solution)/shard_map/all_gather | solution.py:15
  7.9 159.5 %reduce-scatter.4.cloned.1.call-start = ((), (), s32[]{:S(2)}) async-start(), calls=%async_computation.5 | async-start | bytes 9437184 | tf_op jit(solution)/shard_map/reduce_scatter | solution.py:16
  77.7 137.3 %all-gather.6.cloned.1.call-start = ((), (), s32[]{:S(2)}) async-start(), calls=%async_computation.6 | async-start | bytes 4718592 | tf_op jit(solution)/shard_map/all_gather | solution.py:22
  169.5 126.2 %reduce-scatter.6.cloned.1.call-start = ((), (), s32[]{:S(2)}) async-start(), calls=%async_computation.7 | async-start | bytes 5242880 | tf_op jit(solution)/shard_map/reduce_scatter | solution.py:23
  244.2 184.1 %all-reduce.3.cloned.1.call-start = ((), (), s32[]{:S(2)}) async-start(), calls=%async_computation.8 | async-start | bytes 524288 | tf_op jit(solution)/shard_map/psum | solution.py:36
  295.8 194.6 %copy-start = (f32[1024,256]{0,1:T(8,128)S(1)}, f32[1024,256]{0,1:T(8,128)}, u32[]{:S(2)}) copy-start(f32[1024,256]{0,1:T(8,128)} %reduce-scatter.6.cloned.1.call-done) | copy-start | bytes 3145732
  299.1 245.9 %all-gather.8.cloned.1.call-start = ((), (), s32[]{:S(2)}) async-start(), calls=%async_computation.9 | async-start | bytes 5242880 | tf_op jit(solution)/shard_map/all_gather | solution.py:39
  493.3 102.9 %reduce-scatter.8.cloned.1.call-start = ((), (), s32[]{:S(2)}) async-start(), calls=%async_computation.10 | async-start | bytes 1179648 | tf_op jit(solution)/shard_map/reduce_scatter | solution.py:40
  597.7 8.7 %all-to-all-start = ((f32[32,4,256]{2,1,0:T(4,128)}), f32[32,4,256]{2,1,0:T(4,128)S(1)}, u32[]{:S(2)}, u32[]{:S(2)}) async-start(f32[32,4,256]{2,1,0:T(4,128)} %reshape.30), calls=%async_computation.3 | async-start | bytes 262144 | tf_op jit(solution)/shard_map/all_to_all | solution.py:51
Sparse Core Ops, SparseCore 0:
  9.8 37.8 all-gather.3
  77.9 89.5 reduce-scatter.3
  169.6 45.3 all-gather.5
  244.3 51.3 reduce-scatter.5
  301.7 126.5 all-reduce.2
  493.4 51.6 all-gather.7
  563.5 32.6 reduce-scatter.7
where the time goes:
time: 614 us
  waiting for transfers between devices  444 us (72%)
  matrix products  83.1 us (14%)
  other arithmetic  58 us (9%)
  between operations  15.6 us (3%)
  local copies, waits for them, and re-layouts  8.87 us (1%)
    psum x1, waiting for transfers between devices, body(): small_gram = lax.psum(own_gram, ('row', 'col'))  129 us
    reduce_scatter x1, waiting for transfers between devices, body(): lax.psum_scatter(lax.dot_general(gram, own_rows, contract_rows, preferred...  89.6 us
    all_gather x1, waiting for transfers between devices, body(): block_basis = lax.all_gather(basis_cols, 'col', axis=0, tiled=True)  51.7 us
    reduce_scatter x1, waiting for transfers between devices, body(): lax.psum_scatter(jnp.dot(gram, col_rows, preferred_element_type=jnp.float...  51.5 us
    all_gather x1, waiting for transfers between devices, body(): col_rows = lax.all_gather(first_image, 'row', axis=0, tiled=True)  45.4 us
    all_gather x1, waiting for transfers between devices, body(): own_rows = lax.all_gather(start_basis, 'col', axis=0, tiled=True)  39.8 us
    another operation x6, other arithmetic, body(): factor = jnp.linalg.cholesky(small_gram)  34 us
    reduce_scatter x1, waiting for transfers between devices, body(): lax.psum_scatter(lax.dot_general(block_basis, slab, contract_rows, precis...  32.8 us
  transfers between devices with their start and end apart: 8, of which 8 were waited for; matrix products, arithmetic and copies ran while one was open for 0% of the time, Pallas kernels for 0%

commit v1 on v0

--- a/solution.py
+++ b/solution.py
@@ -33,7 +33,11 @@
         precision=highest,
         preferred_element_type=jnp.float32,
     )
-    small_gram = lax.psum(own_gram, ("row", "col"))
+
+    def rest_slots(point):
+        return jnp.sum(lax.all_gather(point, ("row", "col")), axis=0)
+
+    small_gram = rest_slots(own_gram)
     factor = jnp.linalg.cholesky(small_gram)
     basis_cols = jax.scipy.linalg.solve_triangular(factor, second_image.T, lower=True).T
     block_basis = lax.all_gather(basis_cols, "col", axis=0, tiled=True)

time: 614 us -> 564 us (0.919)
  waiting for transfers between devices: 444 us -> 392 us
    psum x1 -> x0, waiting for transfers between devices: 129 us -> none  [body(): small_gram = lax.psum(own_gram, ('row', 'col'))]
    all_gather x0 -> x1, waiting for transfers between devices: none -> 77 us  [rest_slots(): return jnp.sum(lax.all_gather(point, ('row', 'col')), axis=0)]
where the time goes in v1:
time: 564 us
  waiting for transfers between devices  392 us (70%)
  matrix products  83.2 us (15%)
  other arithmetic  61 us (11%)
  between operations  15.6 us (3%)
  local copies, waits for them, and re-layouts  7.92 us (1%)
    reduce_scatter x1, waiting for transfers between devices, body(): lax.psum_scatter(lax.dot_general(gram, own_rows, contract_rows, preferred...  89.6 us
    all_gather x1, waiting for transfers between devices, rest_slots(): return jnp.sum(lax.all_gather(point, ('row', 'col')), axis=0)  77 us
    reduce_scatter x1, waiting for transfers between devices, body(): lax.psum_scatter(jnp.dot(gram, col_rows, preferred_element_type=jnp.float...  51.5 us
    all_gather x1, waiting for transfers between devices, body(): block_basis = lax.all_gather(basis_cols, 'col', axis=0, tiled=True)  51.3 us
    all_gather x1, waiting for transfers between devices, body(): col_rows = lax.all_gather(first_image, 'row', axis=0, tiled=True)  45.4 us
    all_gather x1, waiting for transfers between devices, body(): own_rows = lax.all_gather(start_basis, 'col', axis=0, tiled=True)  39.8 us
    another operation x6, other arithmetic, body(): factor = jnp.linalg.cholesky(small_gram)  34 us
    reduce_scatter x1, waiting for transfers between devices, body(): lax.psum_scatter(lax.dot_general(block_basis, slab, contract_rows, precis...  32.8 us
  transfers between devices with their start and end apart: 8, of which 8 were waited for; matrix products, arithmetic and copies ran while one was open for 0% of the time, Pallas kernels for 0%

profile of v1, /device:TPU:0, one launch (start us, length us, event | category | flops | bytes accessed | tf_op | source)
XLA Modules:
  0.0 563.7 jit_solution(6558482097479738117)
XLA Ops:
  7.2 0.0 all-gather.6.cloned.1.call-start
  7.2 0.7 all-gather.6.cloned.1.call-update
  7.9 0.0 reduce-scatter.4.cloned.1.call-start
  7.9 39.8 %all-gather.6.cloned.1.call-done = bf16[4096,256]{1,0:T(8,128)(2,1)} async-done(((bf16[1024,256]{1,0:T(8,128)(2,1)}), bf16[4096,256]{1,0:T(8,128)(2,1)}) %all-gather.6.cloned.1.call-update) | async-done | bytes 2097168 | tf_op jit(solution)/shard_map/all_gather | solution.py:15
  47.8 30.0 %fusion.9 = f32[8192,256]{1,0:T(8,128)} fusion(bf16[4096,8192]{1,0:T(8,128)(2,1)} %param.3, bf16[4096,256]{1,0:T(8,128)(2,1)} %all-gather.6.cloned.1.call-done), kind=kOutput, calls=%fused_computation.32 | convolution fusion | flops 17179869184 | bytes 77594624 | tf_op jit(solution)/shard_map/dot_general | solution.py:17
  77.7 0.0 reduce-scatter.4.cloned.1.call-update
  77.7 0.0 all-gather.8.cloned.1.call-start
  77.8 89.6 %reduce-scatter.4.cloned.1.call-done = f32[1024,256]{1,0:T(8,128)} async-done(((f32[8192,256]{1,0:T(8,128)}), f32[1024,256]{1,0:T(8,128)}) %reduce-scatter.4.cloned.1.call-update) | async-done | bytes 1048592 | tf_op jit(solution)/shard_map/reduce_scatter | solution.py:16
  167.4 2.1 convert_element_type.3
  169.5 0.0 all-gather.8.cloned.1.call-update
  169.5 0.0 reduce-scatter.6.cloned.1.call-start
  169.6 45.4 %all-gather.8.cloned.1.call-done = bf16[8192,256]{1,0:T(8,128)(2,1)} async-done(((bf16[1024,256]{1,0:T(8,128)(2,1)}), bf16[8192,256]{1,0:T(8,128)(2,1)}) %all-gather.8.cloned.1.call-update) | async-done | bytes 4194320 | tf_op jit(solution)/shard_map/all_gather | solution.py:22
  215.0 29.2 %convolution_bitcast_fusion = f32[4096,256]{0,1:T(8,128)} fusion(bf16[8192,256]{1,0:T(8,128)(2,1)} %all-gather.8.cloned.1.call-done, bf16[4096,8192]{1,0:T(8,128)(2,1)} %param.3), kind=kOutput, calls=%fused_computation.2 | convolution fusion | flops 17179869184 | bytes 75497472 | tf_op jit(solution)/shard_map/dot_general | solution.py:24
  244.2 0.0 reduce-scatter.6.cloned.1.call-update
  244.2 0.0 all-gather.12.cloned.1.call-start
  244.3 51.5 %reduce-scatter.6.cloned.1.call-done = f32[1024,256]{0,1:T(8,128)} async-done(((f32[4096,256]{0,1:T(8,128)}), f32[1024,256]{0,1:T(8,128)}) %reduce-scatter.6.cloned.1.call-update) | async-done | bytes 1048592 | tf_op jit(solution)/shard_map/reduce_scatter | solution.py:23
  295.8 0.0 copy-start
  295.8 3.5 fusion.10
  299.3 0.0 all-gather.12.cloned.1.call-update
  299.3 0.2 all-gather.10.cloned.1.call-start
  299.5 77.0 %all-gather.12.cloned.1.call-done = f32[8192,256]{1,0:T(8,128)} async-done(((f32[256,256]{1,0:T(8,128)}), f32[8192,256]{1,0:T(8,128)}) %all-gather.12.cloned.1.call-update) | async-done | bytes 8388624 | tf_op jit(solution)/shard_map/all_gather | solution.py:38
  376.5 3.9 reduce_sum.9
  380.5 0.1 copy.8
  380.6 11.7 %cholesky.50 = f32[128,128]{1,0:T(8,128)S(1)} custom-call(f32[128,128]{1,0:T(8,128)S(1)} %cholesky.118), custom_call_target="Cholesky" | custom-call | tf_op jit(solution)/shard_map/jit(cholesky)/cholesky | solution.py:41
  392.4 9.8 %custom-call.15 = f32[1,128,128]{1,2,0:T(8,128)S(1)} custom-call(f32[1,128,128]{2,1,0:T(8,128)S(1)} %get-tuple-element.27), custom_call_target="InvertDiagBlocksLowerTriangular" | custom-call | tf_op jit(solution)/shard_map/jit(cholesky)/cholesky | solution.py:41
  402.2 0.2 constant_dynamic-update-slice_fusion.1
  402.4 0.3 convolution_subtract_fusion.1
  402.7 11.7 %cholesky.105 = f32[128,128]{1,0:T(8,128)S(1)} custom-call(f32[128,128]{1,0:T(8,128)S(1)} %convolution_subtract_fusion.1), custom_call_target="Cholesky" | custom-call | tf_op jit(solution)/shard_map/jit(cholesky)/cholesky | solution.py:41
  414.5 0.7 compare_reduce_fusion
  416.6 0.1 triangular_solve.57
  416.6 4.3 while.1
  416.8 0.6 fusion.25
  417.4 1.4 bitcast_dynamic-update-slice_fusion.2
  418.9 0.6 fusion.25
  419.5 1.4 bitcast_dynamic-update-slice_fusion.2
  420.9 19.7 %custom-call.16 = f32[2,128,128]{1,2,0:T(8,128)S(1)} custom-call(f32[2,128,128]{2,1,0:T(8,128)S(1)} %get-tuple-element.9), custom_call_target="InvertDiagBlocksLowerTriangular" | custom-call | tf_op jit(solution)/shard_map/jit(_solve_triangular)/triangular_solve | solution.py:42
  440.6 0.0 copy-done
  440.6 0.6 fusion
  441.3 0.6 convolution_subtract_fusion
  441.8 0.6 fusion.4
  442.5 1.0 maximum_bitcast_fusion
  443.5 0.0 all-gather.10.cloned.1.call-update
  443.5 0.0 reduce-scatter.8.cloned.1.call-start
  443.6 51.3 %all-gather.10.cloned.1.call-done = f32[4096,256]{0,1:T(8,128)} async-done(((f32[1024,256]{0,1:T(8,128)}), f32[4096,256]{0,1:T(8,128)}) %all-gather.10.cloned.1.call-update) | async-done | bytes 4194320 | tf_op jit(solution)/shard_map/all_gather | solution.py:43
  494.9 18.3 %fusion.11 = f32[256,1024]{1,0:T(8,128)} fusion(f32[4096,256]{0,1:T(8,128)} %all-gather.10.cloned.1.call-done, f32[4096,1024]{1,0:T(8,128)} %param.5), kind=kOutput, calls=%fused_computation.34 | convolution fusion | flops 12884901888 | bytes 22020096 | tf_op jit(solution)/shard_map/dot_general | solution.py:45
  513.2 0.0 reduce-scatter.8.cloned.1.call-update
  513.2 32.8 %reduce-scatter.8.cloned.1.call-done = f32[32,1024]{1,0:T(8,128)} async-done(((f32[256,1024]{1,0:T(8,128)}), f32[32,1024]{1,0:T(8,128)}) %reduce-scatter.8.cloned.1.call-update) | async-done | bytes 131088 | tf_op jit(solution)/shard_map/reduce_scatter | solution.py:44
  546.0 1.6 reshape.30
  547.6 3.6 all-to-all-start
  551.2 0.1 broadcast_multiply_fusion
  551.3 1.3 copy.10
  552.6 3.6 all-to-all-done
  556.2 0.7 reshape.31
  (11 shorter events, 0.2 us)
Async XLA Ops:
  7.2 40.6 %all-gather.6.cloned.1.call-start = ((), (), s32[]{:S(2)}) async-start(), calls=%async_computation.4 | async-start | bytes 2621440 | tf_op jit(solution)/shard_map/all_gather | solution.py:15
  7.9 159.5 %reduce-scatter.4.cloned.1.call-start = ((), (), s32[]{:S(2)}) async-start(), calls=%async_computation.5 | async-start | bytes 9437184 | tf_op jit(solution)/shard_map/reduce_scatter | solution.py:16
  77.7 137.3 %all-gather.8.cloned.1.call-start = ((), (), s32[]{:S(2)}) async-start(), calls=%async_computation.6 | async-start | bytes 4718592 | tf_op jit(solution)/shard_map/all_gather | solution.py:22
  169.5 126.2 %reduce-scatter.6.cloned.1.call-start = ((), (), s32[]{:S(2)}) async-start(), calls=%async_computation.7 | async-start | bytes 5242880 | tf_op jit(solution)/shard_map/reduce_scatter | solution.py:23
  244.2 132.3 %all-gather.12.cloned.1.call-start = ((), (), s32[]{:S(2)}) async-start(), calls=%async_computation.10 | async-start | bytes 8650752 | tf_op jit(solution)/shard_map/all_gather | solution.py:38
  295.8 144.8 %copy-start = (f32[1024,256]{0,1:T(8,128)S(1)}, f32[1024,256]{0,1:T(8,128)}, u32[]{:S(2)}) copy-start(f32[1024,256]{0,1:T(8,128)} %reduce-scatter.6.cloned.1.call-done) | copy-start | bytes 3145732
  299.3 195.6 %all-gather.10.cloned.1.call-start = ((), (), s32[]{:S(2)}) async-start(), calls=%async_computation.8 | async-start | bytes 5242880 | tf_op jit(solution)/shard_map/all_gather | solution.py:43
  443.5 102.4 %reduce-scatter.8.cloned.1.call-start = ((), (), s32[]{:S(2)}) async-start(), calls=%async_computation.9 | async-start | bytes 1179648 | tf_op jit(solution)/shard_map/reduce_scatter | solution.py:44
  547.6 8.6 %all-to-all-start = ((f32[32,4,256]{2,1,0:T(4,128)}), f32[32,4,256]{2,1,0:T(4,128)S(1)}, u32[]{:S(2)}, u32[]{:S(2)}) async-start(f32[32,4,256]{2,1,0:T(4,128)} %reshape.30), calls=%async_computation.3 | async-start | bytes 262144 | tf_op jit(solution)/shard_map/all_to_all | solution.py:55
Sparse Core Ops, SparseCore 0:
  9.8 37.8 all-gather.5
  77.9 89.5 reduce-scatter.3
  169.6 45.3 all-gather.7
  244.3 51.3 reduce-scatter.5
  299.4 77.0 all-gather.11
  443.7 51.1 all-gather.9
  513.3 32.6 reduce-scatter.7
